TPU v7x, 512 devices: a whole 4x4x16 slice. The times are simulated.
512 devices in a mesh: blk: 16 (over z), pen: 32 (over x, y, core).
Axes of the slice: x: 4, y: 4, z: 16, core: 2. Of those that a mesh axis runs over, the one named last changes fastest.
Arguments:
- state: bfloat16 [16, 2, 32, 512, 512], P('blk', None, None, 'pen'), may hold values from -6 to 6
- inverse_x: bfloat16 [16, 2, 512, 512], P('blk')
- inverse_y: bfloat16 [16, 2, 512, 512], P('blk')
- rates: float32 [16, 3], P('blk'), may hold values from 0.05 to 0.4
- partner: int32 [16, 2], P('blk'), may hold values from 0 to 15
- face_side: int32 [16, 2], P('blk'), may hold values from 0 to 1
- orient: int32 [16, 2], P('blk'), may hold values from 0 to 1
- offset: int32 [16, 2], P('blk'), may hold values from 0 to 31
Outputs:
- relaxed: bfloat16 [16, 2, 32, 512, 512], P('blk', None, None, 'pen')
All inputs are finite; a program needn't handle non-finite values.
Results may differ from a plain program's by a relative error of at most 0.0058.
Values may be sent and summed in bfloat16 or wider, within the bound.
No kernel may reach another device: no remote copies, remote signals or barrier semaphores. Data moves between devices by JAX's collectives and lax.ppermute only.
A program may use at most 64 MiB of HBM per device.

v0:
```python
import jax
import jax.numpy as jnp
from jax import lax
from jax.sharding import PartitionSpec as P

STEPS = 2


def plane_ghosts(layers, partner_row, side_row, orient_row, offset_row, tile_rows):
    blocks = lax.all_gather(layers[None], "blk", axis=0, tiled=True)
    lines = layers.shape[-1]
    rows_y = jnp.arange(lines, dtype=jnp.int32)
    result = []
    for which in range(2):
        piece = lax.dynamic_index_in_dim(blocks, partner_row[which], 0, keepdims=False)
        segment = lax.dynamic_index_in_dim(piece, side_row[which], 0, keepdims=False)
        mirrored = jnp.where(orient_row[which] == 1, lines - 1 - rows_y, rows_y)
        take_at = (mirrored + offset_row[which] * tile_rows) % lines
        result.append(jnp.take(segment, take_at, axis=-1))
    return result


def local(state, inverse_x, inverse_y, rates, partner, face_side, orient, offset):
    magnet = state[0]
    inv_x = inverse_x[0]
    inv_y = inverse_y[0]
    rate_row = rates[0]
    first_col = inv_x[:, :, 0].astype(jnp.float32)
    last_col = inv_x[:, :, -1].astype(jnp.float32)
    tile_rows = magnet.shape[2]
    planes = lax.all_to_all(magnet, "pen", split_axis=1, concat_axis=2, tiled=True)
    for repeat in range(STEPS):
        layers = jnp.stack([planes[..., 0], planes[..., -1]], axis=0)
        ghosts = plane_ghosts(layers, partner[0], face_side[0], orient[0], offset[0], tile_rows)
        interior = jnp.einsum("fax,fzyx->fzya", inv_x, planes, preferred_element_type=jnp.float32)
        edges = first_col[:, None, None, :] * ghosts[0].astype(jnp.float32)[..., None]
        edges = edges + last_col[:, None, None, :] * ghosts[1].astype(jnp.float32)[..., None]
        swept_x = (interior + edges).astype(jnp.bfloat16)
        swept_y = jnp.einsum("fcy,fzyx->fzcx", inv_y, swept_x, preferred_element_type=jnp.float32)
        proton = swept_y[0]
        carbon = swept_y[1]
        new_proton = proton - (rate_row[0] * proton + rate_row[2] * carbon)
        new_carbon = carbon - (rate_row[1] * carbon + rate_row[2] * proton)
        planes = jnp.stack([new_proton, new_carbon]).astype(jnp.bfloat16)
    magnet = lax.all_to_all(planes, "pen", split_axis=2, concat_axis=1, tiled=True)
    return magnet[None]


def solution(mesh):
    return jax.shard_map(
        local,
        mesh=mesh,
        in_specs=(
            P("blk", None, None, "pen", None),
            P("blk", None, None, None),
            P("blk", None, None, None),
            P("blk", None),
            P("blk", None),
            P("blk", None),
            P("blk", None),
            P("blk", None),
        ),
        out_specs=P("blk", None, None, "pen", None),
        check_vma=False,
    )
```

profile of v0, /device:TPU:1, one launch (start us, length us, event | category | flops | bytes accessed | tf_op | source)
XLA Modules:
  0.0 137.5 jit_solution(13616519110712983959)
XLA Ops:
  0.0 0.0 copy-start
  0.0 0.0 copy-start.9
  0.0 0.0 copy-start.10
  0.0 0.0 copy-start.3
  0.0 0.0 copy-start.1
  0.1 2.4 %copy.81 = bf16[1,2,32,16,512]{4,3,1,2,0:T(8,128)(2,1)} copy(bf16[1,2,32,16,512]{4,3,2,1,0:T(8,128)(2,1)} %param.10) | data formatting | bytes 2097152 | tf_op args[0]
  2.5 10.5 %all-to-all-start = ((bf16[2,32,16,512]{3,2,0,1:T(8,128)(2,1)}), bf16[2,32,16,512]{3,2,0,1:T(8,128)(2,1)S(1)}, u32[]{:S(2)}, u32[]{:S(2)}) async-start(bf16[2,32,16,512]{3,2,0,1:T(8,128)(2,1)} %bitcast.95), calls=%async_computation | async-start | bytes 2097152 | tf_op jit(solution)/shard_map/all_to_all | solution.py:31
  12.9 0.0 copy-done.7
  13.0 0.6 fusion.19
  16.1 0.0 copy-done.8
  16.1 0.6 fusion.18
  21.5 0.0 copy-done.9
  21.5 0.6 fusion.16
  23.4 0.0 copy-done.10
  23.4 0.7 fusion.17
  25.4 0.0 copy-start.5
  25.5 0.7 fusion.15
  26.2 0.3 convert_reduce_fusion.1
  26.5 3.5 %all-to-all-done = bf16[2,32,16,512]{3,2,0,1:T(8,128)(2,1)S(1)} async-done(((bf16[2,32,16,512]{3,2,0,1:T(8,128)(2,1)}), bf16[2,32,16,512]{3,2,0,1:T(8,128)(2,1)S(1)}, u32[]{:S(2)}, u32[]{:S(2)}) %all-to-all-start) | async-done | bytes 1048608 | tf_op jit(solution)/shard_map/all_to_all | solution.py:31
  29.9 0.1 copy.54
  30.0 0.3 slice_reduce_fusion.1
  30.4 26.5 %all-gather = bf16[32,2,1,512]{3,1,2,0:T(2,128)(2,1)S(1)} all-gather(bf16[2,2,1,512]{3,1,2,0:T(2,128)(2,1)S(1)} %pad_maximum_fusion.3), channel_id=2, replica_groups=mesh['blk'=16,'pen'=32] {'blk'}, dimensions={0}, use_global_device_ids=true | all-gather | bytes 69632 | tf_op jit(solution)/shard_map/all_gather | solution.py:10
  56.9 0.2 copy.74
  57.1 1.3 gather_fusion
  58.5 0.1 bitcast_convert_fusion.3
  58.6 0.1 copy.57
  58.7 0.2 copy.75
  58.9 1.3 gather_fusion.1
  60.3 0.1 bitcast_convert_fusion.2
  60.4 0.1 copy.59
  60.5 4.0 %convolution_bitcast_fusion.1 = f32[2,1,512,512]{2,3,0,1:T(8,128)} fusion(bf16[1,2,512,512]{3,2,1,0:T(8,128)(2,1)S(1)} %copy-done, bf16[2,512,512]{2,1,0:T(8,128)(2,1)S(1)} %bitcast.97, f32[2,512]{1,0:T(2,128)S(1)} %copy.59, f32[2,512]{1,0:T(2,128)S(1)} %get-tuple-element.7, f32[2,512]{1,0:T(2,128)S(1)} %copy.57, f32[2,512]{1,0:T(2,128)S(1)} %get-tuple-element.6, ...), kind=kOutput, calls=%fused_computation.7 | convolution fusion | flops 1076363264 | bytes 5259264 | tf_op jit(solution)/shard_map/fcy,fzyx->fzcx/dot_general | solution.py:39
  64.5 3.8 %subtract_convert_fusion.3 = (bf16[1,1,512,512]{2,3,0,1:T(8,128)(2,1)S(1)}, bf16[1,1,512,512]{2,3,0,1:T(8,128)(2,1)S(1)}) fusion(f32[2,1,512,512]{2,3,0,1:T(8,128)} %convolution_bitcast_fusion.1, f32[]{:T(128)} %bitcast.27, f32[]{:T(128)} %bitcast.26, f32[]{:T(128)} %bitcast.30), kind=kLoop, calls=%fused_computation.18 | loop fusion | flops 2621440 | bytes 3145740 | tf_op jit(solution)/shard_map/convert.13
  68.3 0.0 copy-start.2
  68.3 19.7 %all-gather.1 = bf16[32,2,1,512]{3,1,2,0:T(2,128)(2,1)S(1)} all-gather(bf16[2,2,1,512]{3,1,2,0:T(2,128)(2,1)S(1)} %pad_maximum_fusion.4), channel_id=3, replica_groups=mesh['blk'=16,'pen'=32] {'blk'}, dimensions={0}, use_global_device_ids=true | all-gather | bytes 69632 | tf_op jit(solution)/shard_map/all_gather | solution.py:10
  88.1 0.2 copy.76
  88.3 1.3 gather_fusion.2
  89.6 0.7 bitcast_convert_fusion.1
  90.4 0.1 copy.63
  90.5 0.2 copy.77
  90.7 1.3 gather_fusion.3
  92.0 0.7 bitcast_convert_fusion
  92.8 0.1 copy.65
  92.9 3.9 %convolution_bitcast_fusion = f32[2,1,512,512]{2,3,0,1:T(8,128)} fusion(bf16[1,2,512,512]{3,2,1,0:T(8,128)(2,1)S(1)} %copy-done, bf16[1,512,512]{1,2,0:T(8,128)(2,1)S(1)} %bitcast.99, bf16[1,512,512]{1,2,0:T(8,128)(2,1)S(1)} %bitcast.98, f32[2,512]{1,0:T(2,128)S(1)} %copy.65, f32[2,512]{1,0:T(2,128)S(1)} %copy.63, f32[2,512]{1,0:T(2,128)} %copy-done.4, ...), kind=kOutput, calls=%fused_computation.6 | convolution fusion | flops 1076887552 | bytes 5259264 | tf_op jit(solution)/shard_map/fcy,fzyx->fzcx/dot_general | solution.py:39
  96.8 3.8 %subtract_convert_fusion.1 = (bf16[1,1,512,512]{2,3,0,1:T(8,128)(2,1)S(1)}, bf16[1,1,512,512]{2,3,0,1:T(8,128)(2,1)S(1)}) fusion(f32[2,1,512,512]{2,3,0,1:T(8,128)} %convolution_bitcast_fusion, f32[]{:T(128)} %bitcast.27, f32[]{:T(128)} %bitcast.26, f32[]{:T(128)} %bitcast.30), kind=kLoop, calls=%fused_computation.16 | loop fusion | flops 2621440 | bytes 3145740 | tf_op jit(solution)/shard_map/convert.6
  100.6 0.1 pad_maximum_fusion
  100.7 1.0 copy.67
  101.7 34.6 %all_to_all.21 = bf16[2,1,512,512]{3,0,1,2:T(2,128)(2,1)S(1)} all-to-all(bf16[2,1,512,512]{3,0,1,2:T(2,128)(2,1)S(1)} %copy.67), channel_id=1, replica_groups=mesh['blk'=16,'pen'=32] {'pen'}, dimensions={2} | all-to-all | bytes 2097152 | tf_op jit(solution)/shard_map/all_to_all | solution.py:45
  136.3 1.1 copy.68
  (23 shorter events, 0.2 us)
Async XLA Ops:
  0.0 60.5 %copy-start = (bf16[1,2,512,512]{3,2,1,0:T(8,128)(2,1)S(1)}, bf16[1,2,512,512]{3,2,1,0:T(8,128)(2,1)}, u32[]{:S(2)}) copy-start(bf16[1,2,512,512]{3,2,1,0:T(8,128)(2,1)} %param.12) | copy-start | bytes 3145732
  0.0 12.9 %copy-start.7 = (s32[1,2]{1,0:T(1,128)S(1)}, s32[1,2]{1,0:T(1,128)}, u32[]{:S(2)}) copy-start(s32[1,2]{1,0:T(1,128)} %param.14) | copy-start | bytes 28
  0.0 16.1 %copy-start.8 = (s32[1,2]{1,0:T(1,128)S(1)}, s32[1,2]{1,0:T(1,128)}, u32[]{:S(2)}) copy-start(s32[1,2]{1,0:T(1,128)} %param.15) | copy-start | bytes 28
  0.0 21.5 %copy-start.9 = (s32[1,2]{1,0:T(1,128)S(1)}, s32[1,2]{1,0:T(1,128)}, u32[]{:S(2)}) copy-start(s32[1,2]{1,0:T(1,128)} %param.16) | copy-start | bytes 28
  0.0 23.3 %copy-start.10 = (s32[1,2]{1,0:T(1,128)S(1)}, s32[1,2]{1,0:T(1,128)}, u32[]{:S(2)}) copy-start(s32[1,2]{1,0:T(1,128)} %param.17) | copy-start | bytes 28
  0.0 25.5 %copy-start.3 = (f32[1,3]{1,0:T(1,128)S(1)}, f32[1,3]{1,0:T(1,128)}, u32[]{:S(2)}) copy-start(f32[1,3]{1,0:T(1,128)} %param.13) | copy-start | bytes 40
  0.0 26.1 %copy-start.1 = (bf16[1,2,512,512]{3,2,1,0:T(8,128)(2,1)S(1)}, bf16[1,2,512,512]{3,2,1,0:T(8,128)(2,1)}, u32[]{:S(2)}) copy-start(bf16[1,2,512,512]{3,2,1,0:T(8,128)(2,1)} %param.11) | copy-start | bytes 3145732
  2.5 27.5 %all-to-all-start = ((bf16[2,32,16,512]{3,2,0,1:T(8,128)(2,1)}), bf16[2,32,16,512]{3,2,0,1:T(8,128)(2,1)S(1)}, u32[]{:S(2)}, u32[]{:S(2)}) async-start(bf16[2,32,16,512]{3,2,0,1:T(8,128)(2,1)} %bitcast.95), calls=%async_computation | async-start | bytes 2097152 | tf_op jit(solution)/shard_map/all_to_all | solution.py:31
  25.4 33.5 %copy-start.6 = (pred[512]{0:T(512)(128)(4,1)}, pred[512]{0:T(512)(128)(4,1)S(1)}, u32[]{:S(2)}) copy-start(pred[512]{0:T(512)(128)(4,1)S(1)} %compare_and_fusion.1) | copy-start | bytes 1540
  25.4 34.8 %copy-start.5 = (pred[512]{0:T(512)(128)(4,1)}, pred[512]{0:T(512)(128)(4,1)S(1)}, u32[]{:S(2)}) copy-start(pred[512]{0:T(512)(128)(4,1)S(1)} %compare_and_fusion) | copy-start | bytes 1540
  26.5 34.0 %copy-start.4 = (f32[2,512]{1,0:T(2,128)}, f32[2,512]{1,0:T(2,128)S(1)}, u32[]{:S(2)}) copy-start(f32[2,512]{1,0:T(2,128)S(1)} %get-tuple-element.7) | copy-start | bytes 12292
  68.3 24.6 %copy-start.2 = (bf16[1,2,512,512]{3,2,1,0:T(8,128)(2,1)S(1)}, bf16[1,2,512,512]{3,2,1,0:T(8,128)(2,1)}, u32[]{:S(2)}) copy-start(bf16[1,2,512,512]{3,2,1,0:T(8,128)(2,1)} %param.11) | copy-start | bytes 3145732
where the time goes:
time: 138 us; the launch traced here: 137 us
  blocking collectives  80.9 us (59%)
  local copies, waits for them, and re-layouts  14.7 us (11%)
  starting transfers between devices  10.5 us (8%)
  between operations  10.2 us (7%)
  other arithmetic  9.87 us (7%)
  matrix products  7.85 us (6%)
  waiting for transfers between devices  3.45 us (2%)
    all_gather x2, blocking collectives, plane_ghosts(): blocks = lax.all_gather(layers[None], 'blk', axis=0, tiled=True)  46.3 us
    all_to_all x1, blocking collectives, local(): lax.all_to_all(planes, 'pen', split_axis=2, concat_axis=1, tiled=True)  34.6 us
    all_to_all x1, starting transfers between devices, local(): lax.all_to_all(magnet, 'pen', split_axis=1, concat_axis=2, tiled=True)  10.5 us
    dot_general x2, matrix products, local(): jnp.einsum('fcy,fzyx->fzcx', inv_y, swept_x, preferred_element_type=jnp.f...  7.85 us
    another operation x2, other arithmetic  7.59 us
    gather x4, local copies, waits for them, and re-layouts, plane_ghosts(): result.append(jnp.take(segment, take_at, axis=-1))  5.36 us
    all_to_all x1, waiting for transfers between devices, local(): lax.all_to_all(magnet, 'pen', split_axis=1, concat_axis=2, tiled=True)  3.45 us
    unnamed x28, local copies, waits for them, and re-layouts  3.23 us
  transfers between devices with their start and end apart: 1, of which 1 were waited for; matrix products, arithmetic and copies ran while one was open for 3% of the time, Pallas kernels for 0%

commit v1 on v0

--- a/solution.py
+++ b/solution.py
@@ -7,7 +7,20 @@
 
 
 def plane_ghosts(layers, partner_row, side_row, orient_row, offset_row, tile_rows):
-    blocks = lax.all_gather(layers[None], "blk", axis=0, tiled=True)
+
+    def works_recast(u_in):
+        lanes = lax.axis_size("blk")
+        mid_arr = sorted(((p, (p + 1) % lanes) for p in range(lanes)))
+        n_now = u_in
+        shelf = [n_now]
+        for kk in range(1, lanes):
+            n_now = lax.ppermute(n_now, "blk", mid_arr)
+            shelf.insert(0, n_now)
+        y = jnp.concatenate(shelf, axis=0)
+        outer = lax.axis_index("blk") + 1
+        return jnp.roll(y, shift=outer * u_in.shape[0], axis=0)
+
+    blocks = works_recast(layers[None])
     lines = layers.shape[-1]
     rows_y = jnp.arange(lines, dtype=jnp.int32)
     result = []

time: 138 us -> 287 us (2.08)
  waiting for transfers between devices: 3.45 us -> 104 us
  starting transfers between devices: 10.5 us -> 57.7 us
    ppermute x0 -> x30, waiting for transfers between devices: none -> 104 us  [works_recast(): n_now = lax.ppermute(n_now, 'blk', mid_arr)]
    ppermute x0 -> x30, starting transfers between devices: none -> 57.7 us  [works_recast(): n_now = lax.ppermute(n_now, 'blk', mid_arr)]
    all_gather x2 -> x0, blocking collectives: 46.3 us -> none  [plane_ghosts(): blocks = lax.all_gather(layers[None], 'blk', axis=0, tiled=True)]
    all_to_all x0 -> x1, blocking collectives: none -> 26.7 us  [local(): lax.all_to_all(magnet, 'pen', split_axis=1, concat_axis=2, tiled=True)]
    all_to_all x1, blocking collectives: 34.6 us -> 53.5 us  [local(): lax.all_to_all(planes, 'pen', split_axis=2, concat_axis=1, tiled=True)]
    all_to_all x1 -> x0, starting transfers between devices: 10.5 us -> none  [local(): lax.all_to_all(magnet, 'pen', split_axis=1, concat_axis=2, tiled=True)]
    all_to_all x1 -> x0, waiting for transfers between devices: 3.45 us -> none  [local(): lax.all_to_all(magnet, 'pen', split_axis=1, concat_axis=2, tiled=True)]
    another operation x4 -> x2, other arithmetic: 7.61 us -> 7.53 us
  transfers between devices with their start and end apart: 1 -> 30, of which waited for: 1 -> 29; matrix products, arithmetic and copies ran while one was open for 3% -> 2% of each run, Pallas kernels for 0% -> 0%
where the time goes in v1:
time: 287 us; the launch traced here: 285 us
  waiting for transfers between devices  104 us (36%)
  blocking collectives  80.1 us (28%)
  starting transfers between devices  57.7 us (20%)
  local copies, waits for them, and re-layouts  14.6 us (5%)
  other arithmetic  11 us (4%)
  between operations  10.5 us (4%)
  matrix products  7.27 us (3%)
    ppermute x30, waiting for transfers between devices, works_recast(): n_now = lax.ppermute(n_now, 'blk', mid_arr)  104 us
    ppermute x30, starting transfers between devices, works_recast(): n_now = lax.ppermute(n_now, 'blk', mid_arr)  57.7 us
    all_to_all x1, blocking collectives, local(): lax.all_to_all(planes, 'pen', split_axis=2, concat_axis=1, tiled=True)  53.5 us
    all_to_all x1, blocking collectives, local(): lax.all_to_all(magnet, 'pen', split_axis=1, concat_axis=2, tiled=True)  26.7 us
    another operation x2, other arithmetic  7.53 us
    dot_general x2, matrix products, local(): jnp.einsum('fcy,fzyx->fzcx', inv_y, swept_x, preferred_element_type=jnp.f...  7.27 us
  transfers between devices with their start and end apart: 30, of which 29 were waited for; matrix products, arithmetic and copies ran while one was open for 2% of the time, Pallas kernels for 0%

profile of v1, /device:TPU:1, one launch (start us, length us, event | category | flops | bytes accessed | tf_op | source)
XLA Modules:
  0.0 285.3 jit_solution(652110809813496359)
XLA Ops:
  1.4 26.7 %all_to_all.21 = bf16[2,32,16,512]{3,2,0,1:T(8,128)(2,1)S(1)} all-to-all(bf16[2,32,16,512]{3,2,0,1:T(8,128)(2,1)S(1)} %bitcast.102), channel_id=1, replica_groups=mesh['blk'=16,'pen'=32] {'pen'}, dimensions={1} | all-to-all | bytes 2097152 | tf_op jit(solution)/shard_map/all_to_all | solution.py:44
  28.5 2.3 collective-permute-start
  30.8 8.6 %collective-permute-done = bf16[1,2,2,1,512]{4,2,1,3,0:T(2,128)(2,1)S(1)} collective-permute-done((bf16[1,2,2,1,512]{4,2,1,3,0:T(2,128)(2,1)S(1)}, bf16[1,2,2,1,512]{4,2,1,3,0:T(2,128)(2,1)S(1)}, u32[]{:S(2)}, u32[]{:S(2)}) %collective-permute-start) | collective-permute-done | bytes 4128 | tf_op jit(solution)/shard_map/ppermute | solution.py:17
  39.4 1.9 collective-permute-start.1
  41.3 3.6 %collective-permute-done.1 = bf16[1,2,2,1,512]{4,2,1,3,0:T(2,128)(2,1)S(1)} collective-permute-done((bf16[1,2,2,1,512]{4,2,1,3,0:T(2,128)(2,1)S(1)}, bf16[1,2,2,1,512]{4,2,1,3,0:T(2,128)(2,1)S(1)}, u32[]{:S(2)}, u32[]{:S(2)}) %collective-permute-start.1) | collective-permute-done | bytes 4128 | tf_op jit(solution)/shard_map/ppermute | solution.py:17
  45.0 1.9 collective-permute-start.2
  46.9 3.6 %collective-permute-done.2 = bf16[1,2,2,1,512]{4,2,1,3,0:T(2,128)(2,1)S(1)} collective-permute-done((bf16[1,2,2,1,512]{4,2,1,3,0:T(2,128)(2,1)S(1)}, bf16[1,2,2,1,512]{4,2,1,3,0:T(2,128)(2,1)S(1)}, u32[]{:S(2)}, u32[]{:S(2)}) %collective-permute-start.2) | collective-permute-done | bytes 4128 | tf_op jit(solution)/shard_map/ppermute | solution.py:17
  50.5 1.9 collective-permute-start.3
  52.4 3.6 %collective-permute-done.3 = bf16[1,2,2,1,512]{4,2,1,3,0:T(2,128)(2,1)S(1)} collective-permute-done((bf16[1,2,2,1,512]{4,2,1,3,0:T(2,128)(2,1)S(1)}, bf16[1,2,2,1,512]{4,2,1,3,0:T(2,128)(2,1)S(1)}, u32[]{:S(2)}, u32[]{:S(2)}) %collective-permute-start.3) | collective-permute-done | bytes 4128 | tf_op jit(solution)/shard_map/ppermute | solution.py:17
  56.1 1.9 collective-permute-start.4
  58.0 3.6 %collective-permute-done.4 = bf16[1,2,2,1,512]{4,2,1,3,0:T(2,128)(2,1)S(1)} collective-permute-done((bf16[1,2,2,1,512]{4,2,1,3,0:T(2,128)(2,1)S(1)}, bf16[1,2,2,1,512]{4,2,1,3,0:T(2,128)(2,1)S(1)}, u32[]{:S(2)}, u32[]{:S(2)}) %collective-permute-start.4) | collective-permute-done | bytes 4128 | tf_op jit(solution)/shard_map/ppermute | solution.py:17
  64.4 2.7 collective-permute-done.5
  69.7 3.0 %collective-permute-done.6 = bf16[1,2,2,1,512]{4,2,1,3,0:T(2,128)(2,1)S(1)} collective-permute-done((bf16[1,2,2,1,512]{4,2,1,3,0:T(2,128)(2,1)S(1)}, bf16[1,2,2,1,512]{4,2,1,3,0:T(2,128)(2,1)S(1)}, u32[]{:S(2)}, u32[]{:S(2)}) %collective-permute-start.6) | collective-permute-done | bytes 4128 | tf_op jit(solution)/shard_map/ppermute | solution.py:17
  72.7 1.9 collective-permute-start.7
  75.2 3.0 %collective-permute-done.7 = bf16[1,2,2,1,512]{4,2,1,3,0:T(2,128)(2,1)S(1)} collective-permute-done((bf16[1,2,2,1,512]{4,2,1,3,0:T(2,128)(2,1)S(1)}, bf16[1,2,2,1,512]{4,2,1,3,0:T(2,128)(2,1)S(1)}, u32[]{:S(2)}, u32[]{:S(2)}) %collective-permute-start.7) | collective-permute-done | bytes 4128 | tf_op jit(solution)/shard_map/ppermute | solution.py:17
  80.8 3.0 %collective-permute-done.8 = bf16[1,2,2,1,512]{4,2,1,3,0:T(2,128)(2,1)S(1)} collective-permute-done((bf16[1,2,2,1,512]{4,2,1,3,0:T(2,128)(2,1)S(1)}, bf16[1,2,2,1,512]{4,2,1,3,0:T(2,128)(2,1)S(1)}, u32[]{:S(2)}, u32[]{:S(2)}) %collective-permute-start.8) | collective-permute-done | bytes 4128 | tf_op jit(solution)/shard_map/ppermute | solution.py:17
  86.3 3.0 %collective-permute-done.9 = bf16[1,2,2,1,512]{4,2,1,3,0:T(2,128)(2,1)S(1)} collective-permute-done((bf16[1,2,2,1,512]{4,2,1,3,0:T(2,128)(2,1)S(1)}, bf16[1,2,2,1,512]{4,2,1,3,0:T(2,128)(2,1)S(1)}, u32[]{:S(2)}, u32[]{:S(2)}) %collective-permute-start.9) | collective-permute-done | bytes 4128 | tf_op jit(solution)/shard_map/ppermute | solution.py:17
  89.4 1.9 collective-permute-start.10
  96.9 3.6 %collective-permute-done.11 = bf16[1,2,2,1,512]{4,2,1,3,0:T(2,128)(2,1)S(1)} collective-permute-done((bf16[1,2,2,1,512]{4,2,1,3,0:T(2,128)(2,1)S(1)}, bf16[1,2,2,1,512]{4,2,1,3,0:T(2,128)(2,1)S(1)}, u32[]{:S(2)}, u32[]{:S(2)}) %collective-permute-start.11) | collective-permute-done | bytes 4128 | tf_op jit(solution)/shard_map/ppermute | solution.py:17
  100.5 1.9 collective-permute-start.12
  102.4 3.6 %collective-permute-done.12 = bf16[1,2,2,1,512]{4,2,1,3,0:T(2,128)(2,1)S(1)} collective-permute-done((bf16[1,2,2,1,512]{4,2,1,3,0:T(2,128)(2,1)S(1)}, bf16[1,2,2,1,512]{4,2,1,3,0:T(2,128)(2,1)S(1)}, u32[]{:S(2)}, u32[]{:S(2)}) %collective-permute-start.12) | collective-permute-done | bytes 4128 | tf_op jit(solution)/shard_map/ppermute | solution.py:17
  107.9 3.6 %collective-permute-done.13 = bf16[1,2,2,1,512]{4,2,1,3,0:T(2,128)(2,1)S(1)} collective-permute-done((bf16[1,2,2,1,512]{4,2,1,3,0:T(2,128)(2,1)S(1)}, bf16[1,2,2,1,512]{4,2,1,3,0:T(2,128)(2,1)S(1)}, u32[]{:S(2)}, u32[]{:S(2)}) %collective-permute-start.13) | collective-permute-done | bytes 4128 | tf_op jit(solution)/shard_map/ppermute | solution.py:17
  126.7 3.4 %convolution_bitcast_fusion.1 = f32[2,1,512,512]{2,3,0,1:T(8,128)} fusion(bf16[1,2,512,512]{3,2,1,0:T(8,128)(2,1)S(1)} %copy-done, bf16[2,512,512]{2,1,0:T(8,128)(2,1)S(1)} %bitcast.104, f32[2,512]{1,0:T(2,128)S(1)} %copy.123, f32[2,512]{1,0:T(2,128)} %get-tuple-element.8, f32[2,512]{1,0:T(2,128)} %copy.121, f32[2,512]{1,0:T(2,128)} %get-tuple-element.6, ...), kind=kOutput, calls=%fused_computation.7 | convolution fusion | flops 1076363264 | bytes 5259264 | tf_op jit(solution)/shard_map/fcy,fzyx->fzcx/dot_general | solution.py:52
  130.1 3.8 %subtract_convert_fusion.3 = (bf16[1,1,512,512]{2,3,0,1:T(8,128)(2,1)S(1)}, bf16[1,1,512,512]{2,3,0,1:T(8,128)(2,1)S(1)}) fusion(f32[2,1,512,512]{2,3,0,1:T(8,128)} %convolution_bitcast_fusion.1, f32[]{:T(128)} %bitcast.27, f32[]{:T(128)} %bitcast.26, f32[]{:T(128)} %bitcast.30), kind=kLoop, calls=%fused_computation.18 | loop fusion | flops 2621440 | bytes 3145740 | tf_op jit(solution)/shard_map/convert.13
  133.9 1.9 collective-permute-start.15
  135.8 3.6 %collective-permute-done.15 = bf16[1,2,2,1,512]{4,2,1,3,0:T(2,128)(2,1)S(1)} collective-permute-done((bf16[1,2,2,1,512]{4,2,1,3,0:T(2,128)(2,1)S(1)}, bf16[1,2,2,1,512]{4,2,1,3,0:T(2,128)(2,1)S(1)}, u32[]{:S(2)}, u32[]{:S(2)}) %collective-permute-start.15) | collective-permute-done | bytes 4128 | tf_op jit(solution)/shard_map/ppermute | solution.py:17
  139.5 1.9 collective-permute-start.16
  141.4 3.6 %collective-permute-done.16 = bf16[1,2,2,1,512]{4,2,1,3,0:T(2,128)(2,1)S(1)} collective-permute-done((bf16[1,2,2,1,512]{4,2,1,3,0:T(2,128)(2,1)S(1)}, bf16[1,2,2,1,512]{4,2,1,3,0:T(2,128)(2,1)S(1)}, u32[]{:S(2)}, u32[]{:S(2)}) %collective-permute-start.16) | collective-permute-done | bytes 4128 | tf_op jit(solution)/shard_map/ppermute | solution.py:17
  147.0 3.6 %collective-permute-done.17 = bf16[1,2,2,1,512]{4,2,1,3,0:T(2,128)(2,1)S(1)} collective-permute-done((bf16[1,2,2,1,512]{4,2,1,3,0:T(2,128)(2,1)S(1)}, bf16[1,2,2,1,512]{4,2,1,3,0:T(2,128)(2,1)S(1)}, u32[]{:S(2)}, u32[]{:S(2)}) %collective-permute-start.17) | collective-permute-done | bytes 4128 | tf_op jit(solution)/shard_map/ppermute | solution.py:17
  152.5 3.7 %collective-permute-done.18 = bf16[1,2,2,1,512]{4,2,1,3,0:T(2,128)(2,1)S(1)} collective-permute-done((bf16[1,2,2,1,512]{4,2,1,3,0:T(2,128)(2,1)S(1)}, bf16[1,2,2,1,512]{4,2,1,3,0:T(2,128)(2,1)S(1)}, u32[]{:S(2)}, u32[]{:S(2)}) %collective-permute-start.18) | collective-permute-done | bytes 4128 | tf_op jit(solution)/shard_map/ppermute | solution.py:17
  158.1 3.6 %collective-permute-done.19 = bf16[1,2,2,1,512]{4,2,1,3,0:T(2,128)(2,1)S(1)} collective-permute-done((bf16[1,2,2,1,512]{4,2,1,3,0:T(2,128)(2,1)S(1)}, bf16[1,2,2,1,512]{4,2,1,3,0:T(2,128)(2,1)S(1)}, u32[]{:S(2)}, u32[]{:S(2)}) %collective-permute-start.19) | collective-permute-done | bytes 4128 | tf_op jit(solution)/shard_map/ppermute | solution.py:17
  161.7 1.9 collective-permute-start.20
  163.7 3.6 %collective-permute-done.20 = bf16[1,2,2,1,512]{4,2,1,3,0:T(2,128)(2,1)S(1)} collective-permute-done((bf16[1,2,2,1,512]{4,2,1,3,0:T(2,128)(2,1)S(1)}, bf16[1,2,2,1,512]{4,2,1,3,0:T(2,128)(2,1)S(1)}, u32[]{:S(2)}, u32[]{:S(2)}) %collective-permute-start.20) | collective-permute-done | bytes 4128 | tf_op jit(solution)/shard_map/ppermute | solution.py:17
  169.2 3.6 %collective-permute-done.21 = bf16[1,2,2,1,512]{4,2,1,3,0:T(2,128)(2,1)S(1)} collective-permute-done((bf16[1,2,2,1,512]{4,2,1,3,0:T(2,128)(2,1)S(1)}, bf16[1,2,2,1,512]{4,2,1,3,0:T(2,128)(2,1)S(1)}, u32[]{:S(2)}, u32[]{:S(2)}) %collective-permute-start.21) | collective-permute-done | bytes 4128 | tf_op jit(solution)/shard_map/ppermute | solution.py:17
  174.8 3.6 %collective-permute-done.22 = bf16[1,2,2,1,512]{4,2,1,3,0:T(2,128)(2,1)S(1)} collective-permute-done((bf16[1,2,2,1,512]{4,2,1,3,0:T(2,128)(2,1)S(1)}, bf16[1,2,2,1,512]{4,2,1,3,0:T(2,128)(2,1)S(1)}, u32[]{:S(2)}, u32[]{:S(2)}) %collective-permute-start.22) | collective-permute-done | bytes 4128 | tf_op jit(solution)/shard_map/ppermute | solution.py:17
  178.4 1.9 collective-permute-start.23
  180.3 3.6 %collective-permute-done.23 = bf16[1,2,2,1,512]{4,2,1,3,0:T(2,128)(2,1)S(1)} collective-permute-done((bf16[1,2,2,1,512]{4,2,1,3,0:T(2,128)(2,1)S(1)}, bf16[1,2,2,1,512]{4,2,1,3,0:T(2,128)(2,1)S(1)}, u32[]{:S(2)}, u32[]{:S(2)}) %collective-permute-start.23) | collective-permute-done | bytes 4128 | tf_op jit(solution)/shard_map/ppermute | solution.py:17
  185.9 3.8 %collective-permute-done.24 = bf16[1,2,2,1,512]{4,2,1,3,0:T(2,128)(2,1)S(1)} collective-permute-done((bf16[1,2,2,1,512]{4,2,1,3,0:T(2,128)(2,1)S(1)}, bf16[1,2,2,1,512]{4,2,1,3,0:T(2,128)(2,1)S(1)}, u32[]{:S(2)}, u32[]{:S(2)}) %collective-permute-start.24) | collective-permute-done | bytes 4128 | tf_op jit(solution)/shard_map/ppermute | solution.py:17
  189.7 1.9 collective-permute-start.25
  191.6 3.6 %collective-permute-done.25 = bf16[1,2,2,1,512]{4,2,1,3,0:T(2,128)(2,1)S(1)} collective-permute-done((bf16[1,2,2,1,512]{4,2,1,3,0:T(2,128)(2,1)S(1)}, bf16[1,2,2,1,512]{4,2,1,3,0:T(2,128)(2,1)S(1)}, u32[]{:S(2)}, u32[]{:S(2)}) %collective-permute-start.25) | collective-permute-done | bytes 4128 | tf_op jit(solution)/shard_map/ppermute | solution.py:17
  197.2 3.6 %collective-permute-done.26 = bf16[1,2,2,1,512]{4,2,1,3,0:T(2,128)(2,1)S(1)} collective-permute-done((bf16[1,2,2,1,512]{4,2,1,3,0:T(2,128)(2,1)S(1)}, bf16[1,2,2,1,512]{4,2,1,3,0:T(2,128)(2,1)S(1)}, u32[]{:S(2)}, u32[]{:S(2)}) %collective-permute-start.26) | collective-permute-done | bytes 4128 | tf_op jit(solution)/shard_map/ppermute | solution.py:17
  202.7 3.6 %collective-permute-done.27 = bf16[1,2,2,1,512]{4,2,1,3,0:T(2,128)(2,1)S(1)} collective-permute-done((bf16[1,2,2,1,512]{4,2,1,3,0:T(2,128)(2,1)S(1)}, bf16[1,2,2,1,512]{4,2,1,3,0:T(2,128)(2,1)S(1)}, u32[]{:S(2)}, u32[]{:S(2)}) %collective-permute-start.27) | collective-permute-done | bytes 4128 | tf_op jit(solution)/shard_map/ppermute | solution.py:17
  206.4 1.9 collective-permute-start.28
  208.3 3.6 %collective-permute-done.28 = bf16[1,2,2,1,512]{4,2,1,3,0:T(2,128)(2,1)S(1)} collective-permute-done((bf16[1,2,2,1,512]{4,2,1,3,0:T(2,128)(2,1)S(1)}, bf16[1,2,2,1,512]{4,2,1,3,0:T(2,128)(2,1)S(1)}, u32[]{:S(2)}, u32[]{:S(2)}) %collective-permute-start.28) | collective-permute-done | bytes 4128 | tf_op jit(solution)/shard_map/ppermute | solution.py:17
  213.8 3.6 %collective-permute-done.29 = bf16[1,2,2,1,512]{4,2,1,3,0:T(2,128)(2,1)S(1)} collective-permute-done((bf16[1,2,2,1,512]{4,2,1,3,0:T(2,128)(2,1)S(1)}, bf16[1,2,2,1,512]{4,2,1,3,0:T(2,128)(2,1)S(1)}, u32[]{:S(2)}, u32[]{:S(2)}) %collective-permute-start.29) | collective-permute-done | bytes 4128 | tf_op jit(solution)/shard_map/ppermute | solution.py:17
  221.9 3.9 %convolution_bitcast_fusion = f32[2,1,512,512]{2,3,0,1:T(8,128)} fusion(bf16[1,2,512,512]{3,2,1,0:T(8,128)(2,1)S(1)} %copy-done, bf16[1,512,512]{1,2,0:T(8,128)(2,1)S(1)} %bitcast.106, bf16[1,512,512]{1,2,0:T(8,128)(2,1)S(1)} %bitcast.105, f32[2,512]{1,0:T(2,128)S(1)} %copy.129, f32[2,512]{1,0:T(2,128)S(1)} %copy.127, f32[2,512]{1,0:T(2,128)} %get-tuple-element.8, ...), kind=kOutput, calls=%fused_computation.6 | convolution fusion | flops 1076887552 | bytes 5259264 | tf_op jit(solution)/shard_map/fcy,fzyx->fzcx/dot_general | solution.py:52
  225.8 3.8 %subtract_convert_fusion.1 = (bf16[1,1,512,512]{2,3,0,1:T(8,128)(2,1)S(1)}, bf16[1,1,512,512]{2,3,0,1:T(8,128)(2,1)S(1)}) fusion(f32[2,1,512,512]{2,3,0,1:T(8,128)} %convolution_bitcast_fusion, f32[]{:T(128)} %bitcast.27, f32[]{:T(128)} %bitcast.26, f32[]{:T(128)} %bitcast.30), kind=kLoop, calls=%fused_computation.16 | loop fusion | flops 2621440 | bytes 3145740 | tf_op jit(solution)/shard_map/convert.6
  230.7 53.5 %all_to_all.22 = bf16[2,1,512,512]{3,0,1,2:T(2,128)(2,1)S(1)} all-to-all(bf16[2,1,512,512]{3,0,1,2:T(2,128)(2,1)S(1)} %copy.131), channel_id=1, replica_groups=mesh['blk'=16,'pen'=32] {'pen'}, dimensions={2} | all-to-all | bytes 2097152 | tf_op jit(solution)/shard_map/all_to_all | solution.py:58
  (104 shorter events, 49.1 us)
Async XLA Ops:
  0.0 126.7 %copy-start = (bf16[1,2,512,512]{3,2,1,0:T(8,128)(2,1)S(1)}, bf16[1,2,512,512]{3,2,1,0:T(8,128)(2,1)}, u32[]{:S(2)}) copy-start(bf16[1,2,512,512]{3,2,1,0:T(8,128)(2,1)} %param.14) | copy-start | bytes 3145732
  1.4 62.1 %copy-start.1 = (bf16[1,2,512,512]{3,2,1,0:T(8,128)(2,1)S(1)}, bf16[1,2,512,512]{3,2,1,0:T(8,128)(2,1)}, u32[]{:S(2)}) copy-start(bf16[1,2,512,512]{3,2,1,0:T(8,128)(2,1)} %param.13) | copy-start | bytes 3145732
  28.1 41.0 %copy-start.2 = (f32[1,3]{1,0:T(1,128)S(1)}, f32[1,3]{1,0:T(1,128)}, u32[]{:S(2)}) copy-start(f32[1,3]{1,0:T(1,128)} %param.15) | copy-start | bytes 40
  28.1 46.5 %copy-start.3 = (s32[1,2]{1,0:T(1,128)S(1)}, s32[1,2]{1,0:T(1,128)}, u32[]{:S(2)}) copy-start(s32[1,2]{1,0:T(1,128)} %param.16) | copy-start | bytes 28
  28.1 52.1 %copy-start.4 = (s32[1,2]{1,0:T(1,128)S(1)}, s32[1,2]{1,0:T(1,128)}, u32[]{:S(2)}) copy-start(s32[1,2]{1,0:T(1,128)} %param.17) | copy-start | bytes 28
  28.1 57.6 %copy-start.5 = (s32[1,2]{1,0:T(1,128)S(1)}, s32[1,2]{1,0:T(1,128)}, u32[]{:S(2)}) copy-start(s32[1,2]{1,0:T(1,128)} %param.18) | copy-start | bytes 28
  28.1 63.2 %copy-start.6 = (s32[1,2]{1,0:T(1,128)S(1)}, s32[1,2]{1,0:T(1,128)}, u32[]{:S(2)}) copy-start(s32[1,2]{1,0:T(1,128)} %param.19) | copy-start | bytes 28
  28.5 10.9 %collective-permute-start = (bf16[1,2,2,1,512]{4,2,1,3,0:T(2,128)(2,1)S(1)}, bf16[1,2,2,1,512]{4,2,1,3,0:T(2,128)(2,1)S(1)}, u32[]{:S(2)}, u32[]{:S(2)}) collective-permute-start(bf16[1,2,2,1,512]{4,2,1,3,0:T(2,128)(2,1)S(1)} %maximum_bitcast_fusion), channel_id=1, source_target_pairs={{0,32},{32,64},{64,96},{96,128},{128,160},{160,192},{192,224},{224... | collective-permute-start | bytes 12296 | tf_op jit(solution)/shard_map/ppermute | solution.py:17
  39.4 5.6 %collective-permute-start.1 = (bf16[1,2,2,1,512]{4,2,1,3,0:T(2,128)(2,1)S(1)}, bf16[1,2,2,1,512]{4,2,1,3,0:T(2,128)(2,1)S(1)}, u32[]{:S(2)}, u32[]{:S(2)}) collective-permute-start(bf16[1,2,2,1,512]{4,2,1,3,0:T(2,128)(2,1)S(1)} %collective-permute-done), channel_id=1, source_target_pairs={{0,32},{32,64},{64,96},{96,128},{128,160},{160,192},{192,224},{224... | collective-permute-start | bytes 12296 | tf_op jit(solution)/shard_map/ppermute | solution.py:17
  45.0 5.6 %collective-permute-start.2 = (bf16[1,2,2,1,512]{4,2,1,3,0:T(2,128)(2,1)S(1)}, bf16[1,2,2,1,512]{4,2,1,3,0:T(2,128)(2,1)S(1)}, u32[]{:S(2)}, u32[]{:S(2)}) collective-permute-start(bf16[1,2,2,1,512]{4,2,1,3,0:T(2,128)(2,1)S(1)} %collective-permute-done.1), channel_id=1, source_target_pairs={{0,32},{32,64},{64,96},{96,128},{128,160},{160,192},{192,224},{224... | collective-permute-start | bytes 12296 | tf_op jit(solution)/shard_map/ppermute | solution.py:17
  50.5 5.6 %collective-permute-start.3 = (bf16[1,2,2,1,512]{4,2,1,3,0:T(2,128)(2,1)S(1)}, bf16[1,2,2,1,512]{4,2,1,3,0:T(2,128)(2,1)S(1)}, u32[]{:S(2)}, u32[]{:S(2)}) collective-permute-start(bf16[1,2,2,1,512]{4,2,1,3,0:T(2,128)(2,1)S(1)} %collective-permute-done.2), channel_id=1, source_target_pairs={{0,32},{32,64},{64,96},{96,128},{128,160},{160,192},{192,224},{224... | collective-permute-start | bytes 12296 | tf_op jit(solution)/shard_map/ppermute | solution.py:17
  56.1 5.6 %collective-permute-start.4 = (bf16[1,2,2,1,512]{4,2,1,3,0:T(2,128)(2,1)S(1)}, bf16[1,2,2,1,512]{4,2,1,3,0:T(2,128)(2,1)S(1)}, u32[]{:S(2)}, u32[]{:S(2)}) collective-permute-start(bf16[1,2,2,1,512]{4,2,1,3,0:T(2,128)(2,1)S(1)} %collective-permute-done.3), channel_id=1, source_target_pairs={{0,32},{32,64},{64,96},{96,128},{128,160},{160,192},{192,224},{224... | collective-permute-start | bytes 12296 | tf_op jit(solution)/shard_map/ppermute | solution.py:17
  61.6 5.6 %collective-permute-start.5 = (bf16[1,2,2,1,512]{4,2,1,3,0:T(2,128)(2,1)S(1)}, bf16[1,2,2,1,512]{4,2,1,3,0:T(2,128)(2,1)S(1)}, u32[]{:S(2)}, u32[]{:S(2)}) collective-permute-start(bf16[1,2,2,1,512]{4,2,1,3,0:T(2,128)(2,1)S(1)} %collective-permute-done.4), channel_id=1, source_target_pairs={{0,32},{32,64},{64,96},{96,128},{128,160},{160,192},{192,224},{224... | collective-permute-start | bytes 12296 | tf_op jit(solution)/shard_map/ppermute | solution.py:17
  67.2 5.6 %collective-permute-start.6 = (bf16[1,2,2,1,512]{4,2,1,3,0:T(2,128)(2,1)S(1)}, bf16[1,2,2,1,512]{4,2,1,3,0:T(2,128)(2,1)S(1)}, u32[]{:S(2)}, u32[]{:S(2)}) collective-permute-start(bf16[1,2,2,1,512]{4,2,1,3,0:T(2,128)(2,1)S(1)} %collective-permute-done.5), channel_id=1, source_target_pairs={{0,32},{32,64},{64,96},{96,128},{128,160},{160,192},{192,224},{224... | collective-permute-start | bytes 12296 | tf_op jit(solution)/shard_map/ppermute | solution.py:17
  72.7 5.6 %collective-permute-start.7 = (bf16[1,2,2,1,512]{4,2,1,3,0:T(2,128)(2,1)S(1)}, bf16[1,2,2,1,512]{4,2,1,3,0:T(2,128)(2,1)S(1)}, u32[]{:S(2)}, u32[]{:S(2)}) collective-permute-start(bf16[1,2,2,1,512]{4,2,1,3,0:T(2,128)(2,1)S(1)} %collective-permute-done.6), channel_id=1, source_target_pairs={{0,32},{32,64},{64,96},{96,128},{128,160},{160,192},{192,224},{224... | collective-permute-start | bytes 12296 | tf_op jit(solution)/shard_map/ppermute | solution.py:17
  78.3 5.6 %collective-permute-start.8 = (bf16[1,2,2,1,512]{4,2,1,3,0:T(2,128)(2,1)S(1)}, bf16[1,2,2,1,512]{4,2,1,3,0:T(2,128)(2,1)S(1)}, u32[]{:S(2)}, u32[]{:S(2)}) collective-permute-start(bf16[1,2,2,1,512]{4,2,1,3,0:T(2,128)(2,1)S(1)} %collective-permute-done.7), channel_id=1, source_target_pairs={{0,32},{32,64},{64,96},{96,128},{128,160},{160,192},{192,224},{224... | collective-permute-start | bytes 12296 | tf_op jit(solution)/shard_map/ppermute | solution.py:17
  83.8 5.6 %collective-permute-start.9 = (bf16[1,2,2,1,512]{4,2,1,3,0:T(2,128)(2,1)S(1)}, bf16[1,2,2,1,512]{4,2,1,3,0:T(2,128)(2,1)S(1)}, u32[]{:S(2)}, u32[]{:S(2)}) collective-permute-start(bf16[1,2,2,1,512]{4,2,1,3,0:T(2,128)(2,1)S(1)} %collective-permute-done.8), channel_id=1, source_target_pairs={{0,32},{32,64},{64,96},{96,128},{128,160},{160,192},{192,224},{224... | collective-permute-start | bytes 12296 | tf_op jit(solution)/shard_map/ppermute | solution.py:17
  89.4 5.6 %collective-permute-start.10 = (bf16[1,2,2,1,512]{4,2,1,3,0:T(2,128)(2,1)S(1)}, bf16[1,2,2,1,512]{4,2,1,3,0:T(2,128)(2,1)S(1)}, u32[]{:S(2)}, u32[]{:S(2)}) collective-permute-start(bf16[1,2,2,1,512]{4,2,1,3,0:T(2,128)(2,1)S(1)} %collective-permute-done.9), channel_id=1, source_target_pairs={{0,32},{32,64},{64,96},{96,128},{128,160},{160,192},{192,224},{224... | collective-permute-start | bytes 12296 | tf_op jit(solution)/shard_map/ppermute | solution.py:17
  94.9 5.6 %collective-permute-start.11 = (bf16[1,2,2,1,512]{4,2,1,3,0:T(2,128)(2,1)S(1)}, bf16[1,2,2,1,512]{4,2,1,3,0:T(2,128)(2,1)S(1)}, u32[]{:S(2)}, u32[]{:S(2)}) collective-permute-start(bf16[1,2,2,1,512]{4,2,1,3,0:T(2,128)(2,1)S(1)} %collective-permute-done.10), channel_id=1, source_target_pairs={{0,32},{32,64},{64,96},{96,128},{128,160},{160,192},{192,224},{224... | collective-permute-start | bytes 12296 | tf_op jit(solution)/shard_map/ppermute | solution.py:17
  100.5 5.6 %collective-permute-start.12 = (bf16[1,2,2,1,512]{4,2,1,3,0:T(2,128)(2,1)S(1)}, bf16[1,2,2,1,512]{4,2,1,3,0:T(2,128)(2,1)S(1)}, u32[]{:S(2)}, u32[]{:S(2)}) collective-permute-start(bf16[1,2,2,1,512]{4,2,1,3,0:T(2,128)(2,1)S(1)} %collective-permute-done.11), channel_id=1, source_target_pairs={{0,32},{32,64},{64,96},{96,128},{128,160},{160,192},{192,224},{224... | collective-permute-start | bytes 12296 | tf_op jit(solution)/shard_map/ppermute | solution.py:17
  106.0 5.6 %collective-permute-start.13 = (bf16[1,2,2,1,512]{4,2,1,3,0:T(2,128)(2,1)S(1)}, bf16[1,2,2,1,512]{4,2,1,3,0:T(2,128)(2,1)S(1)}, u32[]{:S(2)}, u32[]{:S(2)}) collective-permute-start(bf16[1,2,2,1,512]{4,2,1,3,0:T(2,128)(2,1)S(1)} %collective-permute-done.12), channel_id=1, source_target_pairs={{0,32},{32,64},{64,96},{96,128},{128,160},{160,192},{192,224},{224... | collective-permute-start | bytes 12296 | tf_op jit(solution)/shard_map/ppermute | solution.py:17
  111.6 10.1 %collective-permute-start.14 = (bf16[1,2,2,1,512]{4,2,1,3,0:T(2,128)(2,1)S(1)}, bf16[1,2,2,1,512]{4,2,1,3,0:T(2,128)(2,1)S(1)}, u32[]{:S(2)}, u32[]{:S(2)}) collective-permute-start(bf16[1,2,2,1,512]{4,2,1,3,0:T(2,128)(2,1)S(1)} %collective-permute-done.13), channel_id=1, source_target_pairs={{0,32},{32,64},{64,96},{96,128},{128,160},{160,192},{192,224},{224... | collective-permute-start | bytes 12296 | tf_op jit(solution)/shard_map/ppermute | solution.py:17
  133.9 5.6 %collective-permute-start.15 = (bf16[1,2,2,1,512]{4,2,1,3,0:T(2,128)(2,1)S(1)}, bf16[1,2,2,1,512]{4,2,1,3,0:T(2,128)(2,1)S(1)}, u32[]{:S(2)}, u32[]{:S(2)}) collective-permute-start(bf16[1,2,2,1,512]{4,2,1,3,0:T(2,128)(2,1)S(1)} %maximum_bitcast_fusion.1), channel_id=1, source_target_pairs={{0,32},{32,64},{64,96},{96,128},{128,160},{160,192},{192,224},{224... | collective-permute-start | bytes 12296 | tf_op jit(solution)/shard_map/ppermute | solution.py:17
  139.5 5.6 %collective-permute-start.16 = (bf16[1,2,2,1,512]{4,2,1,3,0:T(2,128)(2,1)S(1)}, bf16[1,2,2,1,512]{4,2,1,3,0:T(2,128)(2,1)S(1)}, u32[]{:S(2)}, u32[]{:S(2)}) collective-permute-start(bf16[1,2,2,1,512]{4,2,1,3,0:T(2,128)(2,1)S(1)} %collective-permute-done.15), channel_id=1, source_target_pairs={{0,32},{32,64},{64,96},{96,128},{128,160},{160,192},{192,224},{224... | collective-permute-start | bytes 12296 | tf_op jit(solution)/shard_map/ppermute | solution.py:17
  145.0 5.6 %collective-permute-start.17 = (bf16[1,2,2,1,512]{4,2,1,3,0:T(2,128)(2,1)S(1)}, bf16[1,2,2,1,512]{4,2,1,3,0:T(2,128)(2,1)S(1)}, u32[]{:S(2)}, u32[]{:S(2)}) collective-permute-start(bf16[1,2,2,1,512]{4,2,1,3,0:T(2,128)(2,1)S(1)} %collective-permute-done.16), channel_id=1, source_target_pairs={{0,32},{32,64},{64,96},{96,128},{128,160},{160,192},{192,224},{224... | collective-permute-start | bytes 12296 | tf_op jit(solution)/shard_map/ppermute | solution.py:17
  150.6 5.6 %collective-permute-start.18 = (bf16[1,2,2,1,512]{4,2,1,3,0:T(2,128)(2,1)S(1)}, bf16[1,2,2,1,512]{4,2,1,3,0:T(2,128)(2,1)S(1)}, u32[]{:S(2)}, u32[]{:S(2)}) collective-permute-start(bf16[1,2,2,1,512]{4,2,1,3,0:T(2,128)(2,1)S(1)} %collective-permute-done.17), channel_id=1, source_target_pairs={{0,32},{32,64},{64,96},{96,128},{128,160},{160,192},{192,224},{224... | collective-permute-start | bytes 12296 | tf_op jit(solution)/shard_map/ppermute | solution.py:17
  156.2 5.6 %collective-permute-start.19 = (bf16[1,2,2,1,512]{4,2,1,3,0:T(2,128)(2,1)S(1)}, bf16[1,2,2,1,512]{4,2,1,3,0:T(2,128)(2,1)S(1)}, u32[]{:S(2)}, u32[]{:S(2)}) collective-permute-start(bf16[1,2,2,1,512]{4,2,1,3,0:T(2,128)(2,1)S(1)} %collective-permute-done.18), channel_id=1, source_target_pairs={{0,32},{32,64},{64,96},{96,128},{128,160},{160,192},{192,224},{224... | collective-permute-start | bytes 12296 | tf_op jit(solution)/shard_map/ppermute | solution.py:17
  161.7 5.6 %collective-permute-start.20 = (bf16[1,2,2,1,512]{4,2,1,3,0:T(2,128)(2,1)S(1)}, bf16[1,2,2,1,512]{4,2,1,3,0:T(2,128)(2,1)S(1)}, u32[]{:S(2)}, u32[]{:S(2)}) collective-permute-start(bf16[1,2,2,1,512]{4,2,1,3,0:T(2,128)(2,1)S(1)} %collective-permute-done.19), channel_id=1, source_target_pairs={{0,32},{32,64},{64,96},{96,128},{128,160},{160,192},{192,224},{224... | collective-permute-start | bytes 12296 | tf_op jit(solution)/shard_map/ppermute | solution.py:17
  167.3 5.6 %collective-permute-start.21 = (bf16[1,2,2,1,512]{4,2,1,3,0:T(2,128)(2,1)S(1)}, bf16[1,2,2,1,512]{4,2,1,3,0:T(2,128)(2,1)S(1)}, u32[]{:S(2)}, u32[]{:S(2)}) collective-permute-start(bf16[1,2,2,1,512]{4,2,1,3,0:T(2,128)(2,1)S(1)} %collective-permute-done.20), channel_id=1, source_target_pairs={{0,32},{32,64},{64,96},{96,128},{128,160},{160,192},{192,224},{224... | collective-permute-start | bytes 12296 | tf_op jit(solution)/shard_map/ppermute | solution.py:17
  172.8 5.6 %collective-permute-start.22 = (bf16[1,2,2,1,512]{4,2,1,3,0:T(2,128)(2,1)S(1)}, bf16[1,2,2,1,512]{4,2,1,3,0:T(2,128)(2,1)S(1)}, u32[]{:S(2)}, u32[]{:S(2)}) collective-permute-start(bf16[1,2,2,1,512]{4,2,1,3,0:T(2,128)(2,1)S(1)} %collective-permute-done.21), channel_id=1, source_target_pairs={{0,32},{32,64},{64,96},{96,128},{128,160},{160,192},{192,224},{224... | collective-permute-start | bytes 12296 | tf_op jit(solution)/shard_map/ppermute | solution.py:17
  178.4 5.6 %collective-permute-start.23 = (bf16[1,2,2,1,512]{4,2,1,3,0:T(2,128)(2,1)S(1)}, bf16[1,2,2,1,512]{4,2,1,3,0:T(2,128)(2,1)S(1)}, u32[]{:S(2)}, u32[]{:S(2)}) collective-permute-start(bf16[1,2,2,1,512]{4,2,1,3,0:T(2,128)(2,1)S(1)} %collective-permute-done.22), channel_id=1, source_target_pairs={{0,32},{32,64},{64,96},{96,128},{128,160},{160,192},{192,224},{224... | collective-permute-start | bytes 12296 | tf_op jit(solution)/shard_map/ppermute | solution.py:17
  184.0 5.7 %collective-permute-start.24 = (bf16[1,2,2,1,512]{4,2,1,3,0:T(2,128)(2,1)S(1)}, bf16[1,2,2,1,512]{4,2,1,3,0:T(2,128)(2,1)S(1)}, u32[]{:S(2)}, u32[]{:S(2)}) collective-permute-start(bf16[1,2,2,1,512]{4,2,1,3,0:T(2,128)(2,1)S(1)} %collective-permute-done.23), channel_id=1, source_target_pairs={{0,32},{32,64},{64,96},{96,128},{128,160},{160,192},{192,224},{224... | collective-permute-start | bytes 12296 | tf_op jit(solution)/shard_map/ppermute | solution.py:17
  189.7 5.6 %collective-permute-start.25 = (bf16[1,2,2,1,512]{4,2,1,3,0:T(2,128)(2,1)S(1)}, bf16[1,2,2,1,512]{4,2,1,3,0:T(2,128)(2,1)S(1)}, u32[]{:S(2)}, u32[]{:S(2)}) collective-permute-start(bf16[1,2,2,1,512]{4,2,1,3,0:T(2,128)(2,1)S(1)} %collective-permute-done.24), channel_id=1, source_target_pairs={{0,32},{32,64},{64,96},{96,128},{128,160},{160,192},{192,224},{224... | collective-permute-start | bytes 12296 | tf_op jit(solution)/shard_map/ppermute | solution.py:17
  195.2 5.6 %collective-permute-start.26 = (bf16[1,2,2,1,512]{4,2,1,3,0:T(2,128)(2,1)S(1)}, bf16[1,2,2,1,512]{4,2,1,3,0:T(2,128)(2,1)S(1)}, u32[]{:S(2)}, u32[]{:S(2)}) collective-permute-start(bf16[1,2,2,1,512]{4,2,1,3,0:T(2,128)(2,1)S(1)} %collective-permute-done.25), channel_id=1, source_target_pairs={{0,32},{32,64},{64,96},{96,128},{128,160},{160,192},{192,224},{224... | collective-permute-start | bytes 12296 | tf_op jit(solution)/shard_map/ppermute | solution.py:17
  200.8 5.6 %collective-permute-start.27 = (bf16[1,2,2,1,512]{4,2,1,3,0:T(2,128)(2,1)S(1)}, bf16[1,2,2,1,512]{4,2,1,3,0:T(2,128)(2,1)S(1)}, u32[]{:S(2)}, u32[]{:S(2)}) collective-permute-start(bf16[1,2,2,1,512]{4,2,1,3,0:T(2,128)(2,1)S(1)} %collective-permute-done.26), channel_id=1, source_target_pairs={{0,32},{32,64},{64,96},{96,128},{128,160},{160,192},{192,224},{224... | collective-permute-start | bytes 12296 | tf_op jit(solution)/shard_map/ppermute | solution.py:17
  206.4 5.6 %collective-permute-start.28 = (bf16[1,2,2,1,512]{4,2,1,3,0:T(2,128)(2,1)S(1)}, bf16[1,2,2,1,512]{4,2,1,3,0:T(2,128)(2,1)S(1)}, u32[]{:S(2)}, u32[]{:S(2)}) collective-permute-start(bf16[1,2,2,1,512]{4,2,1,3,0:T(2,128)(2,1)S(1)} %collective-permute-done.27), channel_id=1, source_target_pairs={{0,32},{32,64},{64,96},{96,128},{128,160},{160,192},{192,224},{224... | collective-permute-start | bytes 12296 | tf_op jit(solution)/shard_map/ppermute | solution.py:17
  211.9 5.6 %collective-permute-start.29 = (bf16[1,2,2,1,512]{4,2,1,3,0:T(2,128)(2,1)S(1)}, bf16[1,2,2,1,512]{4,2,1,3,0:T(2,128)(2,1)S(1)}, u32[]{:S(2)}, u32[]{:S(2)}) collective-permute-start(bf16[1,2,2,1,512]{4,2,1,3,0:T(2,128)(2,1)S(1)} %collective-permute-done.28), channel_id=1, source_target_pairs={{0,32},{32,64},{64,96},{96,128},{128,160},{160,192},{192,224},{224... | collective-permute-start | bytes 12296 | tf_op jit(solution)/shard_map/ppermute | solution.py:17
